TPU v7x, 32 devices: a whole 2x2x4 slice. The times are simulated.
32 devices in a mesh: groups: 2 (over x), rows: 16 (over z, y, core).
Axes of the slice: x: 2, y: 2, z: 4, core: 2. Of those that a mesh axis runs over, the one named last changes fastest.
Arguments:
- block_input: bfloat16 [512, 352, 512], P(('groups', 'rows')), parts along dimension 0, may hold values from -6 to 6
- first_pre: bfloat16 [512, 352, 128], P(('groups', 'rows')), parts along dimension 0, may hold values from -6 to 6
- second_pre: bfloat16 [512, 352, 128], P(('groups', 'rows')), parts along dimension 0, may hold values from -6 to 6
- output_pre: bfloat16 [512, 352, 512], P(('groups', 'rows')), parts along dimension 0, may hold values from -6 to 6
- output_grad: bfloat16 [512, 352, 512], P('groups', None, 'rows'), parts along dimension 0, may hold values from -6 to 6
- first_weight: bfloat16 [512, 128], replicated, may hold values from -0.25 to 0.25
- middle_weight: bfloat16 [3, 3, 128, 128], replicated, may hold values from -0.1875 to 0.1875
- last_weight: bfloat16 [128, 512], replicated, may hold values from -0.5 to 0.5
Outputs:
- input_grad: bfloat16 [512, 352, 512], P(('groups', 'rows')), parts along dimension 0
- first_weight_grad: float32 [1024, 128], P(('groups', 'rows')), parts along dimension 0
- middle_weight_grad: float32 [6, 3, 128, 128], P('groups'), parts along dimension 0
- last_weight_grad: float32 [256, 512], P('groups'), parts along dimension 0
There are 2 independent parts, one for each index of `groups`. A program takes and returns all parts, laid end to end along the dimension named above; an argument that names none is the same for every part. Nothing has to cross between parts.
All inputs are finite; a program needn't handle non-finite values.
Results may differ from a plain program's by a relative error of at most 0.0049.
Values may be sent and summed in bfloat16 or wider, within the bound.
No kernel may reach another device: no remote copies, remote signals or barrier semaphores. Data moves between devices by JAX's collectives and lax.ppermute only.
A program may use at most 128 MiB of HBM per device.

v0:
```python
import math
import jax
import jax.numpy as jnp
from jax import lax
from jax.sharding import PartitionSpec as P


def with_halo(value, sides, width):
    for axis, dim in sides:
        size, length = (lax.axis_size(axis), value.shape[dim])
        up = [(i, (i + 1) % size) for i in range(size - 1)]
        down = [(j, i) for i, j in up]
        last = lax.slice_in_dim(value, length - width, length, axis=dim)
        leading = lax.slice_in_dim(value, 0, width, axis=dim)
        before = lax.ppermute(last, axis, up)
        after = lax.ppermute(leading, axis, down)
        value = jnp.concatenate([before, value, after], axis=dim)
    return value


def contract_rows(left, right):
    return lax.dot_general(
        left, right, (((0,), (0,)), ((), ())), preferred_element_type=jnp.float32
    )


def shards(
    block_input,
    first_pre,
    second_pre,
    output_pre,
    output_grad,
    first_weight,
    middle_weight,
    last_weight,
):
    tile_rows, map_cols, channels = block_input.shape
    inner_width = first_pre.shape[2]
    pixels = tile_rows * map_cols
    factor = 1.0 / math.sqrt(pixels * lax.axis_size("rows"))
    spatial = lax.all_to_all(output_grad, "rows", split_axis=0, concat_axis=2, tiled=True)
    masked_out = jnp.where(output_pre > 0, spatial, jnp.zeros_like(spatial))
    second_act = jnp.maximum(second_pre, jnp.zeros_like(second_pre))
    first_act = jnp.maximum(first_pre, jnp.zeros_like(first_pre))
    out_flat = masked_out.reshape(pixels, channels)
    last_part = contract_rows(second_act.reshape(pixels, inner_width), out_flat)
    last_total = lax.psum(last_part, "rows")
    inner = lax.dot_general(
        out_flat, last_weight, (((1,), (1,)), ((), ())), preferred_element_type=jnp.float32
    )
    second_grad = jnp.where(second_pre.reshape(pixels, inner_width) > 0, inner, 0.0).astype(
        jnp.bfloat16
    )
    second_flat = second_grad
    second_grad = second_flat.reshape(tile_rows, map_cols, inner_width)
    act_ext = with_halo(first_act, (("rows", 0),), 1)
    act_padded = jnp.pad(act_ext, ((0, 0), (1, 1), (0, 0)))
    taps = []
    for row_tap in range(3):
        line = []
        for col_tap in range(3):
            window = act_padded[
                row_tap : row_tap + tile_rows, col_tap : col_tap + map_cols
            ].reshape(pixels, inner_width)
            line.append(contract_rows(window, second_flat))
        taps.append(jnp.stack(line))
    middle_part = jnp.stack(taps)
    grad_ext = with_halo(second_grad, (("rows", 0),), 1)
    grad_padded = jnp.pad(grad_ext, ((0, 0), (1, 1), (0, 0)))
    total = jnp.zeros((pixels, inner_width), jnp.float32)
    for row_tap in range(3):
        for col_tap in range(3):
            moved = grad_padded[
                2 - row_tap : 2 - row_tap + tile_rows, 2 - col_tap : 2 - col_tap + map_cols
            ].reshape(pixels, inner_width)
            total = total + lax.dot_general(
                moved,
                middle_weight[row_tap, col_tap],
                (((1,), (1,)), ((), ())),
                preferred_element_type=jnp.float32,
            )
    first_grad = jnp.where(first_pre.reshape(pixels, inner_width) > 0, total, 0.0).astype(
        jnp.bfloat16
    )
    input_flat = block_input.reshape(pixels, channels)
    first_wgrad = (
        lax.psum_scatter(
            contract_rows(input_flat, first_grad), "rows", scatter_dimension=0, tiled=True
        )
        * factor
    )
    back = lax.dot_general(
        first_grad, first_weight, (((1,), (1,)), ((), ())), preferred_element_type=jnp.float32
    )
    input_grad = (
        (back + out_flat.astype(jnp.float32))
        .astype(jnp.bfloat16)
        .reshape(tile_rows, map_cols, channels)
    )
    middle_total = lax.psum(middle_part, "rows")
    return (input_grad, first_wgrad, middle_total * factor, last_total * factor)


def solution(mesh):
    placed = (
        P(("groups", "rows"), None, None),
        P(("groups", "rows"), None, None),
        P(("groups", "rows"), None, None),
        P(("groups", "rows"), None, None),
        P("groups", None, "rows"),
        P(),
        P(),
        P(),
    )
    return jax.shard_map(
        shards,
        mesh=mesh,
        in_specs=placed,
        out_specs=(
            P(("groups", "rows"), None, None),
            P(("groups", "rows"), None),
            P("groups", None, None, None),
            P("groups", None),
        ),
        check_vma=False,
    )
```

profile of v0, /device:TPU:0, one launch (start us, length us, event | category | flops | bytes accessed | tf_op | source)
XLA Modules:
  0.0 376.6 jit_solution(985985323894171516)
XLA Ops:
  7.2 9.7 %copy.21 = bf16[256,352,32]{1,2,0:T(8,128)(2,1)} copy(bf16[256,352,32]{0,2,1:T(8,128)(2,1)} %param.12) | data formatting | bytes 11534336 | tf_op args[4]
  16.8 7.6 %all-to-all-start = ((bf16[256,352,32]{1,2,0:T(8,128)(2,1)}), bf16[256,352,32]{1,2,0:T(8,128)(2,1)}, u32[]{:S(2)}, u32[]{:S(2)}) async-start(bf16[256,352,32]{1,2,0:T(8,128)(2,1)} %copy.21), calls=%async_computation | async-start | bytes 12582912 | tf_op jit(solution)/shard_map/all_to_all | solution.py:41
  24.6 2.4 collective-permute-start.2
  27.0 1.3 collective-permute-start.3
  28.3 1.3 broadcast_compare_fusion.1
  29.6 1.3 broadcast_compare_fusion
  30.9 8.3 %copy.20 = bf16[16,352,512]{1,2,0:T(8,128)(2,1)} copy(bf16[16,352,512]{2,1,0:T(8,128)(2,1)} %param.11) | data formatting | bytes 11534336 | tf_op args[3]
  39.2 1.7 pad_maximum_fusion.1
  41.4 3.9 %fusion.33 = (bf16[16,352,128]{2,1,0:T(8,128)(2,1)}, bf16[16,352,128]{2,1,0:T(8,128)(2,1)}, bf16[16,352,128]{2,1,0:T(8,128)(2,1)}, bf16[16,352,128]{2,1,0:T(8,12...) fusion(bf16[18,354,128]{2,1,0:T(8,128)(2,1)S(1)} %select_maximum_fusion), kind=kLoop, calls=%fused_computation.73 | loop fusion | bytes 17301504 | tf_op jit(solution)/shard_map/slice | solution.py:62
  45.3 93.3 %all-to-all-done = bf16[256,352,32]{1,2,0:T(8,128)(2,1)} async-done(((bf16[256,352,32]{1,2,0:T(8,128)(2,1)}), bf16[256,352,32]{1,2,0:T(8,128)(2,1)}, u32[]{:S(2)}, u32[]{:S(2)}) %all-to-all-start) | async-done | bytes 5767200 | tf_op jit(solution)/shard_map/all_to_all | solution.py:41
  138.6 6.4 %copy.22 = bf16[16,352,16,32]{1,3,2,0:T(8,128)(2,1)} copy(bf16[16,352,16,32]{1,3,0,2:T(8,128)(2,1)} %bitcast.3) | data formatting | bytes 11534336 | tf_op jit(solution)/shard_map/all_to_all | solution.py:41
  145.0 8.0 %compare_select_fusion = bf16[16,352,512]{1,2,0:T(8,128)(2,1)} fusion(bf16[16,352,512]{1,2,0:T(8,128)(2,1)} %copy.20, bf16[16,352,16,32]{1,3,2,0:T(8,128)(2,1)} %copy.22), kind=kLoop, calls=%fused_computation | loop fusion | flops 5767168 | bytes 17301504 | tf_op jit(solution)/shard_map/jit(_where)/select_n | solution.py:42
  153.1 8.5 %copy.23 = bf16[16,352,512]{2,1,0:T(8,128)(2,1)} copy(bf16[16,352,512]{1,2,0:T(8,128)(2,1)} %compare_select_fusion) | data formatting | bytes 11534336 | tf_op jit(solution)/shard_map/jit(_where)/select_n | solution.py:42
  161.6 5.8 %fusion.8 = f32[128,512]{1,0:T(8,128)} fusion(bf16[16,352,512]{1,2,0:T(8,128)(2,1)} %compare_select_fusion, bf16[16,352,128]{2,1,0:T(8,128)(2,1)S(1)} %copy-done.12), kind=kOutput, calls=%fused_computation.28 | convolution fusion | flops 738918400 | bytes 7471104 | tf_op jit(solution)/shard_map/dot_general | solution.py:22
  167.5 1.7 fusion.3
  179.9 2.7 collective-permute-start
  182.6 1.3 collective-permute-start.1
  185.0 8.5 %collective-permute-done.1 = bf16[1,352,128]{2,1,0:T(8,128)(2,1)S(1)} collective-permute-done((bf16[1,352,128]{2,1,0:T(8,128)(2,1)S(1)}, bf16[1,352,128]{2,1,0:T(8,128)(2,1)S(1)}, u32[]{:S(2)}, u32[]{:S(2)}) %collective-permute-start.1) | collective-permute-done | bytes 90144 | tf_op jit(solution)/shard_map/ppermute | solution.py:16
  194.1 2.4 fusion.34
  205.5 6.8 %add_convert_fusion = bf16[5632,512]{1,0:T(8,128)(2,1)} fusion(bf16[5632,512]{1,0:T(8,128)(2,1)} %bitcast.124, bf16[5632,128]{1,0:T(8,128)(2,1)S(1)} %fusion.2, bf16[512,128]{1,0:T(8,128)(2,1)S(1)} %copy-done), kind=kOutput, calls=%fused_computation.1 | convolution fusion | flops 746848256 | bytes 13107200 | tf_op jit(solution)/shard_map/dot_general | solution.py:92
  212.3 97.3 %all-reduce.5.cloned.1.call-done = (f32[3,3,128,128]{3,2,1,0:T(8,128)}, f32[128,512]{1,0:T(8,128)}) async-done(((f32[3,3,128,128]{3,2,1,0:T(8,128)}, f32[128,512]{1,0:T(8,128)}), (f32[3,3,128,128]{3,2,1,0:T(8,128)}, f32[128,512]{1,0:T(8,128)})) %all-reduce.5.cloned.1.call-update) | async-done | bytes 851984 | tf_op jit(solution)/shard_map/psum | solution.py:100
  309.6 1.7 broadcast_multiply_fusion.1
  311.3 1.9 broadcast_multiply_fusion
  313.2 55.1 %reduce-scatter.4.cloned.1.call-done = f32[32,128]{1,0:T(8,128)} async-done(((f32[512,128]{1,0:T(8,128)}), f32[32,128]{1,0:T(8,128)}) %reduce-scatter.4.cloned.1.call-update) | async-done | bytes 16400
  (78 shorter events, 23.3 us)
Async XLA Ops:
  7.2 198.3 %copy-start = (bf16[512,128]{1,0:T(8,128)(2,1)S(1)}, bf16[512,128]{1,0:T(8,128)(2,1)}, u32[]{:S(2)}) copy-start(bf16[512,128]{1,0:T(8,128)(2,1)} %param.13) | copy-start | bytes 393220
  16.8 7.6 %copy-start.2 = (bf16[16,352,128]{2,1,0:T(8,128)(2,1)S(1)}, bf16[16,352,128]{2,1,0:T(8,128)(2,1)}, u32[]{:S(2)}) copy-start(bf16[16,352,128]{2,1,0:T(8,128)(2,1)} %param.9) | copy-start | bytes 4325380
  16.8 121.8 %all-to-all-start = ((bf16[256,352,32]{1,2,0:T(8,128)(2,1)}), bf16[256,352,32]{1,2,0:T(8,128)(2,1)}, u32[]{:S(2)}, u32[]{:S(2)}) async-start(bf16[256,352,32]{1,2,0:T(8,128)(2,1)} %copy.21), calls=%async_computation | async-start | bytes 12582912 | tf_op jit(solution)/shard_map/all_to_all | solution.py:41
  24.4 285.2 %all-reduce.5.cloned.1.call-start = ((), (), s32[]{:S(2)}) async-start(), calls=%async_computation.3 | async-start | bytes 1703936 | tf_op jit(solution)/shard_map/psum | solution.py:100
  24.6 5.0 %copy-start.11 = (bf16[16,352,128]{2,1,0:T(8,128)(2,1)S(1)}, bf16[16,352,128]{2,1,0:T(8,128)(2,1)}, u32[]{:S(2)}) copy-start(bf16[16,352,128]{2,1,0:T(8,128)(2,1)} %param.10) | copy-start | bytes 4325380
  24.6 14.6 %collective-permute-start.2 = (bf16[1,352,128]{2,1,0:T(8,128)(2,1)S(1)}, bf16[1,352,128]{2,1,0:T(8,128)(2,1)S(1)}, u32[]{:S(2)}, u32[]{:S(2)}) collective-permute-start(bf16[1,352,128]{2,1,0:T(8,128)(2,1)S(1)} %get-tuple-element.32), channel_id=1, source_target_pairs={{0,1},{1,2},{2,3},{3,4},{4,5},{5,6},{6,7},{7,8},{8,9},{9,10},{10,1... | collective-permute-start | bytes 270344 | tf_op jit(solution)/shard_map/ppermute | solution.py:15
  27.0 12.2 %collective-permute-start.3 = (bf16[1,352,128]{2,1,0:T(8,128)(2,1)S(1)}, bf16[1,352,128]{2,1,0:T(8,128)(2,1)S(1)}, u32[]{:S(2)}, u32[]{:S(2)}) collective-permute-start(bf16[1,352,128]{2,1,0:T(8,128)(2,1)S(1)} %get-tuple-element.33), channel_id=1, source_target_pairs={{1,0},{2,1},{3,2},{4,3},{5,4},{6,5},{7,6},{8,7},{9,8},{10,9},{11,1... | collective-permute-start | bytes 270344 | tf_op jit(solution)/shard_map/ppermute | solution.py:16
  153.1 8.5 %copy-start.12 = (bf16[16,352,128]{2,1,0:T(8,128)(2,1)S(1)}, bf16[16,352,128]{2,1,0:T(8,128)(2,1)}, u32[]{:S(2)}) copy-start(bf16[16,352,128]{2,1,0:T(8,128)(2,1)} %param.10) | copy-start | bytes 4325380
  161.6 5.8 %copy-start.1 = (bf16[16,352,512]{2,1,0:T(8,128)(2,1)S(1)}, bf16[16,352,512]{2,1,0:T(8,128)(2,1)}, u32[]{:S(2)}) copy-start(bf16[16,352,512]{2,1,0:T(8,128)(2,1)} %copy.23) | copy-start | bytes 17301508
  161.6 5.8 %copy-start.14 = (pred[16,352,128]{2,1,0:T(32,128)(4,1)S(1)}, pred[16,352,128]{2,1,0:T(32,128)(4,1)}, u32[]{:S(2)}) copy-start(pred[16,352,128]{2,1,0:T(32,128)(4,1)} %broadcast_compare_fusion) | copy-start | bytes 2162692
  161.6 5.8 %copy-start.16 = (bf16[128,512]{1,0:T(8,128)(2,1)S(1)}, bf16[128,512]{1,0:T(8,128)(2,1)}, u32[]{:S(2)}) copy-start(bf16[128,512]{1,0:T(8,128)(2,1)} %param.15) | copy-start | bytes 393220
  167.5 1.7 copy-start.10
  169.2 1.4 copy-start.9
  170.5 1.4 copy-start.8
  171.9 1.4 copy-start.7
  173.3 1.4 copy-start.4
  175.2 1.4 copy-start.6
  176.6 1.4 copy-start.5
  179.9 5.2 %collective-permute-start = (bf16[1,352,128]{2,1,0:T(8,128)(2,1)S(1)}, bf16[1,352,128]{2,1,0:T(8,128)(2,1)S(1)}, u32[]{:S(2)}, u32[]{:S(2)}) collective-permute-start(bf16[1,352,128]{2,1,0:T(8,128)(2,1)S(1)} %get-tuple-element.36), channel_id=1, source_target_pairs={{0,1},{1,2},{2,3},{3,4},{4,5},{5,6},{6,7},{7,8},{8,9},{9,10},{10,1... | collective-permute-start | bytes 270344 | tf_op jit(solution)/shard_map/ppermute | solution.py:15
  182.6 11.0 %collective-permute-start.1 = (bf16[1,352,128]{2,1,0:T(8,128)(2,1)S(1)}, bf16[1,352,128]{2,1,0:T(8,128)(2,1)S(1)}, u32[]{:S(2)}, u32[]{:S(2)}) collective-permute-start(bf16[1,352,128]{2,1,0:T(8,128)(2,1)S(1)} %get-tuple-element.37), channel_id=1, source_target_pairs={{1,0},{2,1},{3,2},{4,3},{5,4},{6,5},{7,6},{8,7},{9,8},{10,9},{11,1... | collective-permute-start | bytes 270344 | tf_op jit(solution)/shard_map/ppermute | solution.py:16
  184.8 183.4 %reduce-scatter.4.cloned.1.call-start = ((), (), s32[]{:S(2)}) async-start(), calls=%async_computation.2 | async-start | bytes 278528
  194.1 2.4 copy-start.15
  200.5 2.4 slice-start
  201.6 2.0 slice-start.1
  (2 other events, 2.5 us)
Sparse Core Ops, SparseCore 0:
  184.9 124.6 all-reduce.4
  313.1 55.1 reduce-scatter.3
where the time goes:
time: 378 us; the launch traced here: 377 us
  waiting for transfers between devices  254 us (67%)
  local copies, waits for them, and re-layouts  48.8 us (13%)
  matrix products  25.6 us (7%)
  other arithmetic  18 us (5%)
  starting transfers between devices  15.5 us (4%)
  between operations  14.4 us (4%)
    psum x1, waiting for transfers between devices, shards(): middle_total = lax.psum(middle_part, 'rows')  97.3 us
    all_to_all x1, waiting for transfers between devices, shards(): lax.all_to_all(output_grad, 'rows', split_axis=0, concat_axis=2, tiled=True)  93.3 us
    unnamed x3, waiting for transfers between devices  55.1 us
    unnamed x43, local copies, waits for them, and re-layouts  27.6 us
    dot_general x11, matrix products, contract_rows(): lax.dot_general(left, right, (((0,), (0,)), ((), ())), preferred_element_...  12 us
    ppermute x2, waiting for transfers between devices, with_halo(): after = lax.ppermute(leading, axis, down)  8.54 us
    select_n x1, local copies, waits for them, and re-layouts, shards(): masked_out = jnp.where(output_pre > 0, spatial, jnp.zeros_like(spatial))  8.53 us
    select_n x1, other arithmetic, shards(): masked_out = jnp.where(output_pre > 0, spatial, jnp.zeros_like(spatial))  8.04 us
  transfers between devices with their start and end apart: 7, of which 4 were waited for; matrix products, arithmetic and copies ran while one was open for 10% of the time, Pallas kernels for 0%

commit v1 on v0

--- a/solution.py
+++ b/solution.py
@@ -3,6 +3,23 @@
 import jax.numpy as jnp
 from jax import lax
 from jax.sharding import PartitionSpec as P
+from jax.lax import axis_index, axis_size, ppermute
+
+
+def _expand_series(content, pos_dim, chunk):
+    x_now = content.shape
+    heard = content.reshape(*x_now[:pos_dim], chunk, x_now[pos_dim] // chunk, *x_now[pos_dim + 1 :])
+    val2 = jnp.moveaxis(heard, pos_dim, 0)
+    return val2
+
+
+def targets_name(z, in_dim):
+    z = jnp.moveaxis(z, 0, in_dim)
+    left_arr = z.shape
+    latest = z.reshape(
+        *left_arr[:in_dim], left_arr[in_dim] * left_arr[in_dim + 1], *left_arr[in_dim + 2 :]
+    )
+    return latest
 
 
 def with_halo(value, sides, width):
@@ -38,7 +55,18 @@
     inner_width = first_pre.shape[2]
     pixels = tile_rows * map_cols
     factor = 1.0 / math.sqrt(pixels * lax.axis_size("rows"))
-    spatial = lax.all_to_all(output_grad, "rows", split_axis=0, concat_axis=2, tiled=True)
+    mixed_arr, reached = (axis_size("rows"), axis_index("rows"))
+    fresh = _expand_series(output_grad, 0, mixed_arr)
+    slots = [fresh[reached]]
+    for dd in range(1, mixed_arr):
+        z2 = fresh[reached ^ dd]
+        slots.append(
+            ppermute(
+                z2, axis_name="rows", perm=[(hop_no, hop_no ^ dd) for hop_no in range(mixed_arr)]
+            )
+        )
+    fresh = jnp.stack(slots)[reached ^ jnp.arange(mixed_arr)]
+    spatial = targets_name(fresh, 2)
     masked_out = jnp.where(output_pre > 0, spatial, jnp.zeros_like(spatial))
     second_act = jnp.maximum(second_pre, jnp.zeros_like(second_pre))
     first_act = jnp.maximum(first_pre, jnp.zeros_like(first_pre))

time: 378 us -> 410 us (1.085)
  starting transfers between devices: 15.5 us -> 68.9 us
  waiting for transfers between devices: 254 us -> 209 us
  local copies, waits for them, and re-layouts: 48.8 us -> 72.8 us
    all_to_all x1 -> x0, waiting for transfers between devices: 93.3 us -> none  [shards(): lax.all_to_all(output_grad, 'rows', split_axis=0, concat_axis=2, tiled=True)]
    ppermute x0 -> x15, starting transfers between devices: none -> 61.1 us  [shards(): ppermute(z2, axis_name='rows', perm=[(hop_no, hop_no ^ dd) for hop_no in...]
    ppermute x0 -> x15, waiting for transfers between devices: none -> 49.6 us  [shards(): ppermute(z2, axis_name='rows', perm=[(hop_no, hop_no ^ dd) for hop_no in...]
    unnamed x43 -> x83, local copies, waits for them, and re-layouts: 27.6 us -> 40 us
    ppermute x2, waiting for transfers between devices: 8.54 us -> 0.88 us  [with_halo(): after = lax.ppermute(leading, axis, down)]
    all_to_all x1 -> x0, starting transfers between devices: 7.56 us -> none  [shards(): lax.all_to_all(output_grad, 'rows', split_axis=0, concat_axis=2, tiled=True)]
    gather x0 -> x1, local copies, waits for them, and re-layouts: none -> 6.82 us  [shards(): fresh = jnp.stack(slots)[reached ^ jnp.arange(mixed_arr)]]
    all_to_all x1 -> x0, local copies, waits for them, and re-layouts: 6.43 us -> none  [shards(): lax.all_to_all(output_grad, 'rows', split_axis=0, concat_axis=2, tiled=True)]
  transfers between devices with their start and end apart: 7 -> 21, of which waited for: 4 -> 7; matrix products, arithmetic and copies ran while one was open for 10% -> 14% of each run, Pallas kernels for 0% -> 0%
where the time goes in v1:
time: 410 us; the launch traced here: 409 us
  waiting for transfers between devices  209 us (51%)
  local copies, waits for them, and re-layouts  72.8 us (18%)
  starting transfers between devices  68.9 us (17%)
  matrix products  25.6 us (6%)
  other arithmetic  18.3 us (4%)
  between operations  14.6 us (4%)
    psum x1, waiting for transfers between devices, shards(): middle_total = lax.psum(middle_part, 'rows')  103 us
    ppermute x15, starting transfers between devices, shards(): ppermute(z2, axis_name='rows', perm=[(hop_no, hop_no ^ dd) for hop_no in...  61.1 us
    unnamed x3, waiting for transfers between devices  55.1 us
    ppermute x15, waiting for transfers between devices, shards(): ppermute(z2, axis_name='rows', perm=[(hop_no, hop_no ^ dd) for hop_no in...  49.6 us
    unnamed x83, local copies, waits for them, and re-layouts  40 us
    dot_general x11, matrix products, contract_rows(): lax.dot_general(left, right, (((0,), (0,)), ((), ())), preferred_element_...  12 us
    select_n x1, local copies, waits for them, and re-layouts, shards(): masked_out = jnp.where(output_pre > 0, spatial, jnp.zeros_like(spatial))  8.53 us
  transfers between devices with their start and end apart: 21, of which 7 were waited for; matrix products, arithmetic and copies ran while one was open for 14% of the time, Pallas kernels for 0%

profile of v1, /device:TPU:0, one launch (start us, length us, event | category | flops | bytes accessed | tf_op | source)
XLA Modules:
  0.0 409.0 jit_solution(745274926851184551)
XLA Ops:
  7.3 9.7 %copy.21 = bf16[256,352,32]{1,2,0:T(8,128)(2,1)} copy(bf16[256,352,32]{0,2,1:T(8,128)(2,1)} %param.12) | data formatting | bytes 11534336 | tf_op args[4]
  17.0 5.4 %dynamic-slice_bitcast_fusion = (bf16[16,352,32]{1,2,0:T(8,128)(2,1)S(1)}, bf16[16,352,32]{1,2,0:T(8,128)(2,1)}, bf16[16,352,32]{1,2,0:T(8,128)(2,1)}, bf16[16,3...) fusion(bf16[16,16,352,32]{2,3,1,0:T(8,128)(2,1)} %bitcast.188, ...), kind=kLoop, calls=%fused_computation.60 | loop fusion | bytes 12025920 | tf_op jit(solution)/shard_map/squeeze | solution.py:62
  22.9 2.6 collective-permute-start.1
  31.1 8.4 %copy.20 = bf16[16,352,512]{1,2,0:T(8,128)(2,1)} copy(bf16[16,352,512]{2,1,0:T(8,128)(2,1)} %param.11) | data formatting | bytes 11534336 | tf_op args[3]
  40.8 5.0 %collective-permute-start.3 = (bf16[16,352,32]{1,2,0:T(8,128)(2,1)S(1)}, bf16[16,352,32]{1,2,0:T(8,128)(2,1)S(1)}, u32[]{:S(2)}, u32[]{:S(2)}) collective-permute-start(bf16[16,352,32]{1,2,0:T(8,128)(2,1)S(1)} %copy-done.27), channel_id=1, source_target_pairs={{0,4},{1,5},{2,6},{3,7},{4,0},{5,1},{6,2},{7,3},{8,12},{9,13},{10,... | collective-permute-start | bytes 1081352 | tf_op jit(solution)/shard_map/ppermute | solution.py:64
  48.5 4.0 fusion.34
  52.5 2.9 pad_maximum_fusion.1
  67.6 2.8 collective-permute-start.9
  71.2 19.8 %collective-permute-done.5 = bf16[16,352,32]{1,2,0:T(8,128)(2,1)S(1)} collective-permute-done((bf16[16,352,32]{1,2,0:T(8,128)(2,1)S(1)}, bf16[16,352,32]{1,2,0:T(8,128)(2,1)S(1)}, u32[]{:S(2)}, u32[]{:S(2)}) %collective-permute-start.5) | collective-permute-done | bytes 360480 | tf_op jit(solution)/shard_map/ppermute | solution.py:64
  92.2 2.8 collective-permute-start.11
  95.8 3.7 collective-permute-start.12
  100.4 35.9 %collective-permute-start.13 = (bf16[16,352,32]{1,2,0:T(8,128)(2,1)S(1)}, bf16[16,352,32]{1,2,0:T(8,128)(2,1)S(1)}, u32[]{:S(2)}, u32[]{:S(2)}) collective-permute-start(bf16[16,352,32]{1,2,0:T(8,128)(2,1)S(1)} %copy-done.17), channel_id=1, source_target_pairs={{0,14},{1,15},{2,12},{3,13},{4,10},{5,11},{6,8},{7,9},{8,6},{9,7},... | collective-permute-start | bytes 1081352 | tf_op jit(solution)/shard_map/ppermute | solution.py:64
  137.1 15.2 %collective-permute-done.9 = bf16[16,352,32]{1,2,0:T(8,128)(2,1)S(1)} collective-permute-done((bf16[16,352,32]{1,2,0:T(8,128)(2,1)S(1)}, bf16[16,352,32]{1,2,0:T(8,128)(2,1)S(1)}, u32[]{:S(2)}, u32[]{:S(2)}) %collective-permute-start.9) | collective-permute-done | bytes 360480 | tf_op jit(solution)/shard_map/ppermute | solution.py:64
  153.4 14.3 %collective-permute-done.10 = bf16[16,352,32]{1,2,0:T(8,128)(2,1)S(1)} collective-permute-done((bf16[16,352,32]{1,2,0:T(8,128)(2,1)S(1)}, bf16[16,352,32]{1,2,0:T(8,128)(2,1)S(1)}, u32[]{:S(2)}, u32[]{:S(2)}) %collective-permute-start.10) | collective-permute-done | bytes 360480 | tf_op jit(solution)/shard_map/ppermute | solution.py:64
  171.7 6.8 %gather_fusion = bf16[16,16,352,32]{2,3,1,0:T(8,128)(2,1)} fusion(bf16[16,16,352,32]{2,3,1,0:T(8,128)(2,1)} %bitcast_dynamic-update-slice_fusion, s32[1024]{0:T(1024)S(1)} %pad_clamp_fusion), kind=kCustom, calls=%fused_computation | custom fusion | bytes 11534400 | tf_op jit(solution)/shard_map/gather | solution.py:68
  178.5 3.8 copy.22
  182.3 6.3 %compare_select_fusion = bf16[16,352,512]{1,2,0:T(8,128)(2,1)} fusion(bf16[16,352,512]{1,2,0:T(8,128)(2,1)} %copy.20, bf16[16,352,16,32]{1,3,2,0:T(8,128)(2,1)S(1)} %copy.22), kind=kLoop, calls=%fused_computation.1 | loop fusion | flops 5767168 | bytes 17301504 | tf_op jit(solution)/shard_map/jit(_where)/select_n | solution.py:70
  188.6 8.5 %copy.23 = bf16[16,352,512]{2,1,0:T(8,128)(2,1)} copy(bf16[16,352,512]{1,2,0:T(8,128)(2,1)} %compare_select_fusion) | data formatting | bytes 11534336 | tf_op jit(solution)/shard_map/jit(_where)/select_n | solution.py:70
  197.1 5.8 %fusion.8 = f32[128,512]{1,0:T(8,128)} fusion(bf16[16,352,512]{1,2,0:T(8,128)(2,1)} %compare_select_fusion, bf16[16,352,128]{2,1,0:T(8,128)(2,1)S(1)} %copy-done.14), kind=kOutput, calls=%fused_computation.29 | convolution fusion | flops 738918400 | bytes 7471104 | tf_op jit(solution)/shard_map/dot_general | solution.py:39
  213.5 3.1 collective-permute-start.15
  220.3 2.6 fusion.35
  231.9 6.8 %add_convert_fusion = bf16[5632,512]{1,0:T(8,128)(2,1)} fusion(bf16[5632,512]{1,0:T(8,128)(2,1)} %bitcast.186, bf16[5632,128]{1,0:T(8,128)(2,1)S(1)} %fusion.2, bf16[512,128]{1,0:T(8,128)(2,1)S(1)} %copy-done), kind=kOutput, calls=%fused_computation.2 | convolution fusion | flops 746848256 | bytes 13107200 | tf_op jit(solution)/shard_map/dot_general | solution.py:120
  238.8 103.2 %all-reduce.5.cloned.1.call-done = (f32[3,3,128,128]{3,2,1,0:T(8,128)}, f32[128,512]{1,0:T(8,128)}) async-done(((f32[3,3,128,128]{3,2,1,0:T(8,128)}, f32[128,512]{1,0:T(8,128)}), (f32[3,3,128,128]{3,2,1,0:T(8,128)}, f32[128,512]{1,0:T(8,128)})) %all-reduce.5.cloned.1.call-update) | async-done | bytes 851984 | tf_op jit(solution)/shard_map/psum | solution.py:128
  345.6 55.1 %reduce-scatter.4.cloned.1.call-done = f32[32,128]{1,0:T(8,128)} async-done(((f32[512,128]{1,0:T(8,128)}), f32[32,128]{1,0:T(8,128)}) %reduce-scatter.4.cloned.1.call-update) | async-done | bytes 16400
  (151 shorter events, 59.8 us)
Async XLA Ops:
  7.2 224.7 %copy-start = (bf16[512,128]{1,0:T(8,128)(2,1)S(1)}, bf16[512,128]{1,0:T(8,128)(2,1)}, u32[]{:S(2)}) copy-start(bf16[512,128]{1,0:T(8,128)(2,1)} %param.13) | copy-start | bytes 393220
  7.2 334.8 %all-reduce.5.cloned.1.call-start = ((), (), s32[]{:S(2)}) async-start(), calls=%async_computation.2 | async-start | bytes 1703936 | tf_op jit(solution)/shard_map/psum | solution.py:128
  22.4 33.0 %collective-permute-start = (bf16[16,352,32]{1,2,0:T(8,128)(2,1)}, bf16[16,352,32]{1,2,0:T(8,128)(2,1)}, u32[]{:S(2)}, u32[]{:S(2)}) collective-permute-start(bf16[16,352,32]{1,2,0:T(8,128)(2,1)} %get-tuple-element.32), channel_id=1, source_target_pairs={{0,1},{1,0},{2,3},{3,2},{4,5},{5,4},{6,7},{7,6},{8,9},{9,8},{10,11... | collective-permute-start | bytes 1081352 | tf_op jit(solution)/shard_map/ppermute | solution.py:64
  22.9 36.2 %collective-permute-start.1 = (bf16[16,352,32]{1,2,0:T(8,128)(2,1)}, bf16[16,352,32]{1,2,0:T(8,128)(2,1)}, u32[]{:S(2)}, u32[]{:S(2)}) collective-permute-start(bf16[16,352,32]{1,2,0:T(8,128)(2,1)} %get-tuple-element.31), channel_id=1, source_target_pairs={{0,2},{1,3},{2,0},{3,1},{4,6},{5,7},{6,4},{7,5},{8,10},{9,11},{10,... | collective-permute-start | bytes 1081352 | tf_op jit(solution)/shard_map/ppermute | solution.py:64
  25.5 36.9 %collective-permute-start.2 = (bf16[16,352,32]{1,2,0:T(8,128)(2,1)}, bf16[16,352,32]{1,2,0:T(8,128)(2,1)}, u32[]{:S(2)}, u32[]{:S(2)}) collective-permute-start(bf16[16,352,32]{1,2,0:T(8,128)(2,1)} %get-tuple-element.30), channel_id=1, source_target_pairs={{0,3},{1,2},{2,1},{3,0},{4,7},{5,6},{6,5},{7,4},{8,11},{9,10},{10,... | collective-permute-start | bytes 1081352 | tf_op jit(solution)/shard_map/ppermute | solution.py:64
  26.4 14.4 %collective-permute-start.17 = (bf16[1,352,128]{2,1,0:T(8,128)(2,1)}, bf16[1,352,128]{2,1,0:T(8,128)(2,1)S(1)}, u32[]{:S(2)}, u32[]{:S(2)}) collective-permute-start(bf16[1,352,128]{2,1,0:T(8,128)(2,1)} %get-tuple-element.48), channel_id=1, source_target_pairs={{0,1},{1,2},{2,3},{3,4},{4,5},{5,6},{6,7},{7,8},{8,9},{9,10},{10,1... | collective-permute-start | bytes 270344 | tf_op jit(solution)/shard_map/ppermute | solution.py:32
  28.5 17.3 %collective-permute-start.18 = (bf16[1,352,128]{2,1,0:T(8,128)(2,1)}, bf16[1,352,128]{2,1,0:T(8,128)(2,1)}, u32[]{:S(2)}, u32[]{:S(2)}) collective-permute-start(bf16[1,352,128]{2,1,0:T(8,128)(2,1)} %get-tuple-element.49), channel_id=1, source_target_pairs={{1,0},{2,1},{3,2},{4,3},{5,4},{6,5},{7,6},{8,7},{9,8},{10,9},{11,1... | collective-permute-start | bytes 270344 | tf_op jit(solution)/shard_map/ppermute | solution.py:33
  40.8 25.1 %collective-permute-start.3 = (bf16[16,352,32]{1,2,0:T(8,128)(2,1)S(1)}, bf16[16,352,32]{1,2,0:T(8,128)(2,1)S(1)}, u32[]{:S(2)}, u32[]{:S(2)}) collective-permute-start(bf16[16,352,32]{1,2,0:T(8,128)(2,1)S(1)} %copy-done.27), channel_id=1, source_target_pairs={{0,4},{1,5},{2,6},{3,7},{4,0},{5,1},{6,2},{7,3},{8,12},{9,13},{10,... | collective-permute-start | bytes 1081352 | tf_op jit(solution)/shard_map/ppermute | solution.py:64
  45.8 21.8 %collective-permute-start.4 = (bf16[16,352,32]{1,2,0:T(8,128)(2,1)S(1)}, bf16[16,352,32]{1,2,0:T(8,128)(2,1)S(1)}, u32[]{:S(2)}, u32[]{:S(2)}) collective-permute-start(bf16[16,352,32]{1,2,0:T(8,128)(2,1)S(1)} %copy-done.26), channel_id=1, source_target_pairs={{0,5},{1,4},{2,7},{3,6},{4,1},{5,0},{6,3},{7,2},{8,13},{9,12},{10,... | collective-permute-start | bytes 1081352 | tf_op jit(solution)/shard_map/ppermute | solution.py:64
  55.4 35.6 %collective-permute-start.5 = (bf16[16,352,32]{1,2,0:T(8,128)(2,1)S(1)}, bf16[16,352,32]{1,2,0:T(8,128)(2,1)S(1)}, u32[]{:S(2)}, u32[]{:S(2)}) collective-permute-start(bf16[16,352,32]{1,2,0:T(8,128)(2,1)S(1)} %copy-done.25), channel_id=1, source_target_pairs={{0,6},{1,7},{2,4},{3,5},{4,2},{5,3},{6,0},{7,1},{8,14},{9,15},{10,... | collective-permute-start | bytes 1081352 | tf_op jit(solution)/shard_map/ppermute | solution.py:64
  59.2 31.8 %copy-start.20 = (bf16[16,352,32]{1,2,0:T(8,128)(2,1)S(1)}, bf16[16,352,32]{1,2,0:T(8,128)(2,1)}, u32[]{:S(2)}) copy-start(bf16[16,352,32]{1,2,0:T(8,128)(2,1)} %get-tuple-element.22) | copy-start | bytes 1081348
  59.2 33.0 %collective-permute-start.6 = (bf16[16,352,32]{1,2,0:T(8,128)(2,1)S(1)}, bf16[16,352,32]{1,2,0:T(8,128)(2,1)S(1)}, u32[]{:S(2)}, u32[]{:S(2)}) collective-permute-start(bf16[16,352,32]{1,2,0:T(8,128)(2,1)S(1)} %copy-done.24), channel_id=1, source_target_pairs={{0,7},{1,6},{2,5},{3,4},{4,3},{5,2},{6,1},{7,0},{8,15},{9,14},{10,... | collective-permute-start | bytes 1081352 | tf_op jit(solution)/shard_map/ppermute | solution.py:64
  62.4 33.4 %collective-permute-start.7 = (bf16[16,352,32]{1,2,0:T(8,128)(2,1)S(1)}, bf16[16,352,32]{1,2,0:T(8,128)(2,1)S(1)}, u32[]{:S(2)}, u32[]{:S(2)}) collective-permute-start(bf16[16,352,32]{1,2,0:T(8,128)(2,1)S(1)} %copy-done.23), channel_id=1, source_target_pairs={{0,8},{1,9},{2,10},{3,11},{4,12},{5,13},{6,14},{7,15},{8,0},{9,1},... | collective-permute-start | bytes 1081352 | tf_op jit(solution)/shard_map/ppermute | solution.py:64
  65.9 34.4 %collective-permute-start.8 = (bf16[16,352,32]{1,2,0:T(8,128)(2,1)S(1)}, bf16[16,352,32]{1,2,0:T(8,128)(2,1)S(1)}, u32[]{:S(2)}, u32[]{:S(2)}) collective-permute-start(bf16[16,352,32]{1,2,0:T(8,128)(2,1)S(1)} %copy-done.22), channel_id=1, source_target_pairs={{0,9},{1,8},{2,11},{3,10},{4,13},{5,12},{6,15},{7,14},{8,1},{9,0},... | collective-permute-start | bytes 1081352 | tf_op jit(solution)/shard_map/ppermute | solution.py:64
  67.6 32.8 %copy-start.17 = (bf16[16,352,32]{1,2,0:T(8,128)(2,1)S(1)}, bf16[16,352,32]{1,2,0:T(8,128)(2,1)}, u32[]{:S(2)}) copy-start(bf16[16,352,32]{1,2,0:T(8,128)(2,1)} %get-tuple-element.19) | copy-start | bytes 1081348
  67.6 84.6 %collective-permute-start.9 = (bf16[16,352,32]{1,2,0:T(8,128)(2,1)S(1)}, bf16[16,352,32]{1,2,0:T(8,128)(2,1)S(1)}, u32[]{:S(2)}, u32[]{:S(2)}) collective-permute-start(bf16[16,352,32]{1,2,0:T(8,128)(2,1)S(1)} %copy-done.21), channel_id=1, source_target_pairs={{0,10},{1,11},{2,8},{3,9},{4,14},{5,15},{6,12},{7,13},{8,2},{9,3},... | collective-permute-start | bytes 1081352 | tf_op jit(solution)/shard_map/ppermute | solution.py:64
  91.0 76.7 %collective-permute-start.10 = (bf16[16,352,32]{1,2,0:T(8,128)(2,1)S(1)}, bf16[16,352,32]{1,2,0:T(8,128)(2,1)S(1)}, u32[]{:S(2)}, u32[]{:S(2)}) collective-permute-start(bf16[16,352,32]{1,2,0:T(8,128)(2,1)S(1)} %copy-done.20), channel_id=1, source_target_pairs={{0,11},{1,10},{2,9},{3,8},{4,15},{5,14},{6,13},{7,12},{8,3},{9,2},... | collective-permute-start | bytes 1081352 | tf_op jit(solution)/shard_map/ppermute | solution.py:64
  92.2 76.3 %collective-permute-start.11 = (bf16[16,352,32]{1,2,0:T(8,128)(2,1)S(1)}, bf16[16,352,32]{1,2,0:T(8,128)(2,1)S(1)}, u32[]{:S(2)}, u32[]{:S(2)}) collective-permute-start(bf16[16,352,32]{1,2,0:T(8,128)(2,1)S(1)} %copy-done.19), channel_id=1, source_target_pairs={{0,12},{1,13},{2,14},{3,15},{4,8},{5,9},{6,10},{7,11},{8,4},{9,5},... | collective-permute-start | bytes 1081352 | tf_op jit(solution)/shard_map/ppermute | solution.py:64
  95.8 73.4 %collective-permute-start.12 = (bf16[16,352,32]{1,2,0:T(8,128)(2,1)S(1)}, bf16[16,352,32]{1,2,0:T(8,128)(2,1)S(1)}, u32[]{:S(2)}, u32[]{:S(2)}) collective-permute-start(bf16[16,352,32]{1,2,0:T(8,128)(2,1)S(1)} %copy-done.18), channel_id=1, source_target_pairs={{0,13},{1,12},{2,15},{3,14},{4,9},{5,8},{6,11},{7,10},{8,5},{9,4},... | collective-permute-start | bytes 1081352 | tf_op jit(solution)/shard_map/ppermute | solution.py:64
  100.4 69.7 %collective-permute-start.13 = (bf16[16,352,32]{1,2,0:T(8,128)(2,1)S(1)}, bf16[16,352,32]{1,2,0:T(8,128)(2,1)S(1)}, u32[]{:S(2)}, u32[]{:S(2)}) collective-permute-start(bf16[16,352,32]{1,2,0:T(8,128)(2,1)S(1)} %copy-done.17), channel_id=1, source_target_pairs={{0,14},{1,15},{2,12},{3,13},{4,10},{5,11},{6,8},{7,9},{8,6},{9,7},... | collective-permute-start | bytes 1081352 | tf_op jit(solution)/shard_map/ppermute | solution.py:64
  152.2 18.6 %collective-permute-start.14 = (bf16[16,352,32]{1,2,0:T(8,128)(2,1)S(1)}, bf16[16,352,32]{1,2,0:T(8,128)(2,1)S(1)}, u32[]{:S(2)}, u32[]{:S(2)}) collective-permute-start(bf16[16,352,32]{1,2,0:T(8,128)(2,1)S(1)} %get-tuple-element.18), channel_id=1, source_target_pairs={{0,15},{1,14},{2,13},{3,12},{4,11},{5,10},{6,9},{7,8},{8,7},{9,6},... | collective-permute-start | bytes 1081352 | tf_op jit(solution)/shard_map/ppermute | solution.py:64
  213.5 5.4 %collective-permute-start.15 = (bf16[1,352,128]{2,1,0:T(8,128)(2,1)S(1)}, bf16[1,352,128]{2,1,0:T(8,128)(2,1)S(1)}, u32[]{:S(2)}, u32[]{:S(2)}) collective-permute-start(bf16[1,352,128]{2,1,0:T(8,128)(2,1)S(1)} %get-tuple-element.52), channel_id=1, source_target_pairs={{0,1},{1,2},{2,3},{3,4},{4,5},{5,6},{6,7},{7,8},{8,9},{9,10},{10,1... | collective-permute-start | bytes 270344 | tf_op jit(solution)/shard_map/ppermute | solution.py:32
  216.6 3.2 collective-permute-start.16
  218.9 181.8 %reduce-scatter.4.cloned.1.call-start = ((), (), s32[]{:S(2)}) async-start(), calls=%async_computation.1 | async-start | bytes 278528
  (29 other events, 200.7 us)
Sparse Core Ops, SparseCore 0:
  219.0 122.9 all-reduce.4
  345.5 55.1 reduce-scatter.3
